TPU v7x, 32 devices: a whole 2x2x4 slice. The times are simulated.
32 devices in a mesh: grp: 2 (over x), ep: 16 (over z, y, core).
Axes of the slice: x: 2, y: 2, z: 4, core: 2. Of those that a mesh axis runs over, the one named last changes fastest.
Arguments:
- hidden_in: bfloat16 [2, 1024, 2048], P(None, ('grp', 'ep')), parts along dimension 1, may hold values from -12 to 12
- expert_ids: int32 [2, 1024, 8], P(None, ('grp', 'ep')), parts along dimension 1, may hold values from 0 to 15, all different within a row; in each aligned block of 32 rows (0 to 31, 32 to 63, ..., all dimensions but the last counted through in order) at most 32 rows name the same one
- route_share: int32 [2, 1024, 8], P(None, ('grp', 'ep')), parts along dimension 1, may hold values from 4 to 28
- norm_gain: float32 [2048], replicated, may hold values from 0.1 to 1.9
- gate_weight: bfloat16 [16, 2048, 768], P('ep'), may hold values from -0.125 to 0.125
- up_weight: bfloat16 [16, 2048, 768], P('ep'), may hold values from -0.125 to 0.125
- down_weight: bfloat16 [16, 768, 2048], P('ep'), may hold values from -0.21875 to 0.21875
- exponent_table: int32 [16, 3, 6], P('ep'), may hold values from -2 to 1
Outputs:
- mixed_out: bfloat16 [2, 1024, 2048], P(None, ('grp', 'ep')), parts along dimension 1
There are 2 independent parts, one for each index of `grp`. A program takes and returns all parts, laid end to end along the dimension named above; an argument that names none is the same for every part. Nothing has to cross between parts.
Inputs may be any that keep to these rules, and one draw needn't show every extreme that they name: `expert_ids`: each row names 8 different experts. Within each micro-batch, in each aligned block of 32 rows, no expert is named by more than 32 rows, and in some blocks one expert is named by exactly 32 rows.
All inputs are finite; a program needn't handle non-finite values.
Results may differ from a plain program's by a relative error of at most 0.0044.
Values may be sent and summed in bfloat16 or wider, within the bound.
A program may use at most 64 MiB of HBM per device.

v0:
```python
import jax
import jax.numpy as jnp
from jax import lax
from jax.sharding import PartitionSpec as P

SCALE_GROUP = 128
EXP_DEV = 1


def normalize(rows_in, norm_gain):
    values = rows_in.astype(jnp.float32)
    power = jnp.mean(values * values, axis=-1, keepdims=True)
    return (values * lax.rsqrt(power + 1e-06) * norm_gain).astype(jnp.bfloat16)


def local(
    hidden_in,
    expert_ids,
    route_share,
    norm_gain,
    gate_weight,
    up_weight,
    down_weight,
    exponent_table,
):
    owners = lax.axis_size("ep")
    experts = owners * EXP_DEV
    batches, dev_rows, fanout = expert_ids.shape
    model_width = hidden_in.shape[2]
    capacity = min(dev_rows, 2 * dev_rows * fanout // experts)
    scale_factors = jnp.repeat(jnp.exp2(exponent_table[0].astype(jnp.float32)), SCALE_GROUP, axis=1)
    gate_matrix = gate_weight[0]
    up_matrix = up_weight[0]
    down_mat = down_weight[0]
    slot_ids = jnp.arange(experts * capacity, dtype=jnp.int32)
    expert_range = jnp.arange(experts, dtype=jnp.int32)

    def expert_rows(block_of_rows):
        gate_output = (
            jnp.dot(block_of_rows, gate_matrix, preferred_element_type=jnp.float32)
            * scale_factors[0]
        )
        up_output = (
            jnp.dot(block_of_rows, up_matrix, preferred_element_type=jnp.float32) * scale_factors[1]
        )
        hidden_state = (jax.nn.silu(gate_output) * up_output * scale_factors[2]).astype(
            jnp.bfloat16
        )
        return jnp.dot(hidden_state, down_mat, preferred_element_type=jnp.float32).astype(
            jnp.bfloat16
        )

    def mixing_for(batch):
        flat_ids = expert_ids[batch].reshape(-1)
        onehot = (flat_ids[:, None] == expert_range[None, :]).astype(jnp.int32)
        position = jnp.sum((jnp.cumsum(onehot, axis=0) - 1) * onehot, axis=1)
        slot_of = (flat_ids * capacity + position).reshape(dev_rows, fanout)
        matches = slot_of[:, :, None] == slot_ids[None, None, :]
        shares = route_share[batch].astype(jnp.float32) / 64.0
        mixing = jnp.sum(jnp.where(matches, shares[:, :, None], 0.0), axis=1).astype(jnp.bfloat16)
        picker = jnp.any(matches, axis=1).T.astype(jnp.bfloat16)
        return (mixing, picker)

    def serve(batch_list):
        count = len(batch_list)
        mixings = []
        pickers = []
        for batch in batch_list:
            mixing, picker = mixing_for(batch)
            mixings.append(mixing)
            pickers.append(picker)
        normed_list = [normalize(hidden_in[batch], norm_gain) for batch in batch_list]
        local_rows = normed_list[0]
        local_ids = jnp.concatenate([expert_ids[batch] for batch in batch_list], axis=0)
        all_rows = lax.all_gather(local_rows, "ep", axis=0, tiled=True)
        all_ids = lax.all_gather(local_ids, "ep", axis=0, tiled=True)
        all_rows = all_rows.reshape(owners, count, dev_rows, model_width)
        all_ids = all_ids.reshape(owners, count, dev_rows, fanout)
        owner = lax.axis_index("ep")
        block_base = (jnp.arange(owners, dtype=jnp.int32) * capacity)[:, None]
        ids_here = all_ids[:, 0].reshape(owners, dev_rows * fanout)
        mine = (ids_here == owner).astype(jnp.int32)
        place = jnp.where(mine > 0, block_base + jnp.cumsum(mine, axis=1) - 1, -1)
        place = place.reshape(owners * dev_rows, fanout)
        chooser = jnp.any(place[:, :, None] == slot_ids[None, None, :], axis=1).T.astype(
            jnp.bfloat16
        )
        rows_here = all_rows[:, 0].reshape(owners * dev_rows, model_width)
        built = jnp.dot(chooser, rows_here, preferred_element_type=jnp.float32).astype(jnp.bfloat16)
        buffers = built.reshape(experts, capacity, model_width)
        produced = expert_rows(buffers.reshape(-1, model_width)).reshape(
            experts, count * capacity, model_width
        )
        returned = lax.all_to_all(produced, "ep", split_axis=0, concat_axis=0, tiled=True)
        return (returned, mixings)

    outputs = []
    for batch in range(batches):
        returned, mixings = serve([batch])
        gathered = returned.reshape(experts * capacity, model_width)
        mixed = jnp.dot(mixings[0], gathered, preferred_element_type=jnp.float32)
        outputs.append((hidden_in[batch].astype(jnp.float32) + mixed).astype(jnp.bfloat16))
    return jnp.stack(outputs)


def solution(mesh):
    return jax.shard_map(
        local,
        mesh=mesh,
        in_specs=(
            P(None, ("grp", "ep"), None),
            P(None, ("grp", "ep"), None),
            P(None, ("grp", "ep"), None),
            P(),
            P("ep", None, None),
            P("ep", None, None),
            P("ep", None, None),
            P("ep", None, None),
        ),
        out_specs=P(None, ("grp", "ep"), None),
        check_vma=False,
    )
```

profile of v0, /device:TPU:15, one launch (start us, length us, event | category | flops | bytes accessed | tf_op | source)
XLA Modules:
  0.0 199.0 jit_solution(16054259629744714355)
XLA Ops:
  6.5 0.0 copy-start
  6.5 1.3 fusion.40
  7.8 1.8 fusion.42
  9.6 0.0 all-gather.5.cloned.1.call-update
  9.7 0.0 all-gather.7.cloned.1.call-start
  9.7 0.7 all-gather.7.cloned.1.call-update
  10.4 0.7 fusion.56
  11.1 0.1 copy.36
  11.2 16.5 %all-gather.1 = s32[1,512,8]{2,1,0:T(8,128)S(1)} all-gather(s32[1,32,8]{2,1,0:T(8,128)S(1)} %copy.36), channel_id=3, replica_groups=mesh['grp'=2,'ep'=16] {'ep'}, dimensions={1}, use_global_device_ids=true | all-gather | bytes 17408 | tf_op jit(solution)/shard_map/all_gather | solution.py:76
  27.7 0.7 compare_convert_fusion
  28.4 1.1 reshape.203
  29.5 0.0 copy-start.5
  29.5 0.6 reduce-window.36
  30.1 0.2 slice_reduce_fusion
  30.4 0.1 broadcast_add_fusion
  30.5 0.9 reduce_window_sum.55
  31.3 0.1 copy.35
  31.4 22.5 %all-gather = s32[1,512,8]{2,1,0:T(8,128)S(1)} all-gather(s32[1,32,8]{2,1,0:T(8,128)S(1)} %copy.35), channel_id=2, replica_groups=mesh['grp'=2,'ep'=16] {'ep'}, dimensions={1}, use_global_device_ids=true | all-gather | bytes 17408 | tf_op jit(solution)/shard_map/all_gather | solution.py:76
  53.9 0.7 copy-done.2
  54.6 0.7 compare_convert_fusion.1
  55.3 1.1 reshape.201
  56.4 0.6 reduce-window.30
  57.0 0.2 slice_reduce_fusion.2
  57.2 0.1 broadcast_add_fusion.1
  57.3 0.9 reduce_window_sum.52
  58.2 0.1 add.84
  58.3 0.1 add.85
  58.3 1.9 add_select_fusion.1
  60.3 3.2 %fusion = pred[512,512]{1,0:T(8,128)(4,1)S(1)} fusion(s32[512,8]{1,0:T(8,128)S(1)} %get-tuple-element.13), kind=kLoop, calls=%fused_computation.2 | loop fusion | flops 3932160 | bytes 278528 | tf_op jit(solution)/shard_map/reduce_or | solution.py:85
  63.6 0.1 broadcast_bitcast_fusion.2
  63.6 0.1 broadcast_bitcast_fusion
  63.7 3.0 %convolution_convert_fusion.1 = bf16[512,2048]{1,0:T(8,128)(2,1)S(1)} fusion(pred[512,512]{1,0:T(8,128)(4,1)S(1)} %fusion, bf16[512,2048]{1,0:T(8,128)(2,1)} %all-gather.5.cloned.1.call-done), kind=kOutput, calls=%fused_computation.19 | convolution fusion | flops 1074790400 | bytes 4456448 | tf_op jit(solution)/shard_map/dot_general | solution.py:89
  66.8 2.9 %fusion.8 = f32[512,768]{1,0:T(8,128)} fusion(bf16[512,2048]{1,0:T(8,128)(2,1)S(1)} %convolution_convert_fusion.1, bf16[1,2048,768]{2,1,0:T(8,128)(2,1)S(1)} %copy-done.6), kind=kOutput, calls=%fused_computation.10 | convolution fusion | flops 1610612736 | bytes 6815744 | tf_op jit(solution)/shard_map/dot_general | solution.py:44
  69.7 8.3 %fusion.14 = bf16[512,2048]{1,0:T(8,128)(2,1)} fusion(bf16[1,768,2048]{2,1,0:T(8,128)(2,1)S(1)} %copy-done, f32[512,768]{1,0:T(8,128)} %fusion.8, bf16[512,2048]{1,0:T(8,128)(2,1)} %copy-done.9, bf16[1,2048,768]{2,1,0:T(8,128)(2,1)} %param.12, f32[768]{0:T(1024)S(1)} %get-tuple-element.20, f32[768]{0:T(1024)S(1)} %get-tuple-element.21, ...), kind=kOutput, calls=%fused_computation.16 | convolution fusion | flops 3225812992 | bytes 12067840 | tf_op jit(solution)/shard_map/dot_general | solution.py:49
  78.0 7.2 %all-to-all-start = ((bf16[16,32,2048]{2,1,0:T(8,128)(2,1)}), bf16[16,32,2048]{2,1,0:T(8,128)(2,1)}, u32[]{:S(2)}, u32[]{:S(2)}) async-start(bf16[16,32,2048]{2,1,0:T(8,128)(2,1)} %bitcast.112), calls=%async_computation | async-start | bytes 4194304 | tf_op jit(solution)/shard_map/all_to_all | solution.py:94
  85.2 4.0 %fusion.1 = pred[512,512]{1,0:T(8,128)(4,1)} fusion(s32[512,8]{1,0:T(8,128)S(1)} %copy-done.3), kind=kLoop, calls=%fused_computation.3 | loop fusion | flops 3932160 | bytes 278528 | tf_op jit(solution)/shard_map/reduce_or | solution.py:85
  89.2 8.4 %all-gather.7.cloned.1.call-done = bf16[512,2048]{1,0:T(8,128)(2,1)} async-done(((bf16[32,2048]{1,0:T(8,128)(2,1)}), bf16[512,2048]{1,0:T(8,128)(2,1)}) %all-gather.7.cloned.1.call-update) | async-done | bytes 2097168 | tf_op jit(solution)/shard_map/all_gather | solution.py:75
  97.5 3.1 %convolution_convert_fusion = bf16[512,2048]{1,0:T(8,128)(2,1)S(1)} fusion(pred[512,512]{1,0:T(8,128)(4,1)} %fusion.1, bf16[512,2048]{1,0:T(8,128)(2,1)} %all-gather.7.cloned.1.call-done), kind=kOutput, calls=%fused_computation.18 | convolution fusion | flops 1074790400 | bytes 4456448 | tf_op jit(solution)/shard_map/dot_general | solution.py:89
  100.7 1.3 copy-done.8
  102.0 3.0 %fusion.6 = f32[512,768]{1,0:T(8,128)} fusion(bf16[512,2048]{1,0:T(8,128)(2,1)S(1)} %convolution_convert_fusion, bf16[1,2048,768]{2,1,0:T(8,128)(2,1)S(1)} %copy-done.7), kind=kOutput, calls=%fused_computation.8 | convolution fusion | flops 1610612736 | bytes 6815744 | tf_op jit(solution)/shard_map/dot_general | solution.py:44
  105.0 8.4 %fusion.17 = bf16[512,2048]{1,0:T(8,128)(2,1)} fusion(bf16[1,768,2048]{2,1,0:T(8,128)(2,1)S(1)} %copy-done, f32[512,768]{1,0:T(8,128)} %fusion.6, bf16[512,2048]{1,0:T(8,128)(2,1)} %copy-done.8, bf16[1,2048,768]{2,1,0:T(8,128)(2,1)} %param.12, f32[768]{0:T(1024)S(1)} %get-tuple-element.20, f32[768]{0:T(1024)S(1)} %get-tuple-element.21, ...), kind=kOutput, calls=%fused_computation.17 | convolution fusion | flops 3225812992 | bytes 12067840 | tf_op jit(solution)/shard_map/dot_general | solution.py:49
  113.4 23.4 %all-to-all-done = bf16[16,32,2048]{2,1,0:T(8,128)(2,1)} async-done(((bf16[16,32,2048]{2,1,0:T(8,128)(2,1)}), bf16[16,32,2048]{2,1,0:T(8,128)(2,1)}, u32[]{:S(2)}, u32[]{:S(2)}) %all-to-all-start) | async-done | bytes 2097184 | tf_op jit(solution)/shard_map/all_to_all | solution.py:94
  136.8 5.0 %all-to-all-start.1 = ((bf16[16,32,2048]{2,1,0:T(8,128)(2,1)}), bf16[16,32,2048]{2,1,0:T(8,128)(2,1)}, u32[]{:S(2)}, u32[]{:S(2)}) async-start(bf16[16,32,2048]{2,1,0:T(8,128)(2,1)} %bitcast.111), calls=%async_computation.1 | async-start | bytes 4194304 | tf_op jit(solution)/shard_map/all_to_all | solution.py:94
  141.8 0.1 eq.124
  141.9 0.1 eq.120
  142.0 0.1 eq.140
  142.1 0.1 eq.136
  142.2 0.6 reduce-window.26
  142.8 0.2 slice_reduce_fusion.3
  143.0 0.1 fusion.51
  143.1 0.1 reduce_sum.59
  143.2 0.0 copy-done.4
  143.2 0.1 copy.27
  143.3 0.6 reduce-window.34
  143.9 0.2 slice_reduce_fusion.1
  144.1 0.1 fusion.49
  144.2 0.1 reduce_sum.63
  144.3 0.1 copy.32
  144.4 0.2 select_reduce_fusion.1
  144.6 0.9 select_reduce_fusion
  145.5 2.1 %fusion.23 = bf16[1,32,2048]{2,1,0:T(8,128)(2,1)S(1)} fusion(bf16[512,2048]{1,0:T(8,128)(2,1)} %bitcast.16, bf16[2,32,2048]{2,1,0:T(8,128)(2,1)S(1)} %copy-done.1, bf16[32,512]{1,0:T(8,128)(2,1)S(1)} %select_reduce_fusion.1), kind=kOutput, calls=%fused_computation.25 | convolution fusion | flops 67305472 | bytes 2392064 | tf_op jit(solution)/shard_map/dot_general | solution.py:101
  147.5 41.8 %all-to-all-done.1 = bf16[16,32,2048]{2,1,0:T(8,128)(2,1)} async-done(((bf16[16,32,2048]{2,1,0:T(8,128)(2,1)}), bf16[16,32,2048]{2,1,0:T(8,128)(2,1)}, u32[]{:S(2)}, u32[]{:S(2)}) %all-to-all-start.1) | async-done | bytes 2097184 | tf_op jit(solution)/shard_map/all_to_all | solution.py:94
  189.3 2.1 %fusion.22 = bf16[1,32,2048]{2,1,0:T(8,128)(2,1)S(1)} fusion(bf16[512,2048]{1,0:T(8,128)(2,1)} %bitcast.25, bf16[2,32,2048]{2,1,0:T(8,128)(2,1)S(1)} %copy-done.1, bf16[32,512]{1,0:T(8,128)(2,1)} %select_reduce_fusion), kind=kOutput, calls=%fused_computation.24 | convolution fusion | flops 67305472 | bytes 2392064 | tf_op jit(solution)/shard_map/dot_general | solution.py:101
  191.4 0.7 pad_maximum_fusion
  (38 shorter events, 0.3 us)
Async XLA Ops:
  6.5 63.2 %copy-start = (bf16[1,768,2048]{2,1,0:T(8,128)(2,1)S(1)}, bf16[1,768,2048]{2,1,0:T(8,128)(2,1)}, u32[]{:S(2)}) copy-start(bf16[1,768,2048]{2,1,0:T(8,128)(2,1)} %param.14) | copy-start | bytes 9437188
  6.5 57.2 %all-gather.5.cloned.1.call-start = ((), (), s32[]{:S(2)}) async-start(), calls=%async_computation.2 | async-start | bytes 2228224 | tf_op jit(solution)/shard_map/all_gather | solution.py:75
  9.7 87.9 %all-gather.7.cloned.1.call-start = ((), (), s32[]{:S(2)}) async-start(), calls=%async_computation.3 | async-start | bytes 2228224 | tf_op jit(solution)/shard_map/all_gather | solution.py:75
  29.5 34.0 %copy-start.5 = (s32[1,3,6]{2,0,1:T(1,128)S(1)}, s32[1,3,6]{2,0,1:T(1,128)}, u32[]{:S(2)}) copy-start(s32[1,3,6]{2,0,1:T(1,128)} %param.15) | copy-start | bytes 220
  53.9 0.7 copy-start.2
  63.7 3.0 %copy-start.6 = (bf16[1,2048,768]{2,1,0:T(8,128)(2,1)S(1)}, bf16[1,2048,768]{2,1,0:T(8,128)(2,1)}, u32[]{:S(2)}) copy-start(bf16[1,2048,768]{2,1,0:T(8,128)(2,1)} %param.13) | copy-start | bytes 9437188
  66.8 3.0 %copy-start.9 = (bf16[512,2048]{1,0:T(8,128)(2,1)}, bf16[512,2048]{1,0:T(8,128)(2,1)S(1)}, u32[]{:S(2)}) copy-start(bf16[512,2048]{1,0:T(8,128)(2,1)S(1)} %convolution_convert_fusion.1) | copy-start | bytes 6291460
  78.0 7.2 %copy-start.3 = (s32[512,8]{1,0:T(8,128)S(1)}, s32[512,8]{1,0:T(8,128)}, u32[]{:S(2)}) copy-start(s32[512,8]{1,0:T(8,128)} %get-tuple-element.14) | copy-start | bytes 49156
  78.0 58.8 %all-to-all-start = ((bf16[16,32,2048]{2,1,0:T(8,128)(2,1)}), bf16[16,32,2048]{2,1,0:T(8,128)(2,1)}, u32[]{:S(2)}, u32[]{:S(2)}) async-start(bf16[16,32,2048]{2,1,0:T(8,128)(2,1)} %bitcast.112), calls=%async_computation | async-start | bytes 4194304 | tf_op jit(solution)/shard_map/all_to_all | solution.py:94
  97.5 4.5 %copy-start.7 = (bf16[1,2048,768]{2,1,0:T(8,128)(2,1)S(1)}, bf16[1,2048,768]{2,1,0:T(8,128)(2,1)}, u32[]{:S(2)}) copy-start(bf16[1,2048,768]{2,1,0:T(8,128)(2,1)} %param.13) | copy-start | bytes 9437188
  100.7 1.3 copy-start.8
  136.8 6.4 %copy-start.4 = (s32[2,32,8]{1,2,0:T(8,128)S(1)}, s32[2,32,8]{1,2,0:T(8,128)}, u32[]{:S(2)}) copy-start(s32[2,32,8]{1,2,0:T(8,128)} %param.10) | copy-start | bytes 6148
  136.8 8.7 %copy-start.1 = (bf16[2,32,2048]{2,1,0:T(8,128)(2,1)S(1)}, bf16[2,32,2048]{2,1,0:T(8,128)(2,1)}, u32[]{:S(2)}) copy-start(bf16[2,32,2048]{2,1,0:T(8,128)(2,1)} %param.8) | copy-start | bytes 786436
  136.8 52.5 %all-to-all-start.1 = ((bf16[16,32,2048]{2,1,0:T(8,128)(2,1)}), bf16[16,32,2048]{2,1,0:T(8,128)(2,1)}, u32[]{:S(2)}, u32[]{:S(2)}) async-start(bf16[16,32,2048]{2,1,0:T(8,128)(2,1)} %bitcast.111), calls=%async_computation.1 | async-start | bytes 4194304 | tf_op jit(solution)/shard_map/all_to_all | solution.py:94
Sparse Core Ops, SparseCore 0:
  9.8 41.8 all-gather.4
  53.8 43.6 all-gather.6
where the time goes:
time: 199 us
  waiting for transfers between devices  74.3 us (37%)
  blocking collectives  38.9 us (20%)
  matrix products  32.9 us (17%)
  other arithmetic  18.4 us (9%)
  between operations  13.6 us (7%)
  starting transfers between devices  12.2 us (6%)
  local copies, waits for them, and re-layouts  8.62 us (4%)
    all_to_all x2, waiting for transfers between devices, serve(): lax.all_to_all(produced, 'ep', split_axis=0, concat_axis=0, tiled=True)  65.2 us
    all_gather x2, blocking collectives, serve(): all_ids = lax.all_gather(local_ids, 'ep', axis=0, tiled=True)  38.9 us
    dot_general x2, matrix products, expert_rows(): jnp.dot(hidden_state, down_mat, preferred_element_type=jnp.float32)  16.6 us
    all_to_all x2, starting transfers between devices, serve(): lax.all_to_all(produced, 'ep', split_axis=0, concat_axis=0, tiled=True)  12.2 us
    all_gather x2, waiting for transfers between devices, serve(): all_rows = lax.all_gather(local_rows, 'ep', axis=0, tiled=True)  8.36 us
    reduce_or x2, other arithmetic, serve(): jnp.any(place[:, :, None] == slot_ids[None, None, :], axis=1)  7.21 us
    dot_general x2, matrix products, serve(): jnp.dot(chooser, rows_here, preferred_element_type=jnp.float32)  6.14 us
    dot_general x2, matrix products, expert_rows(): jnp.dot(block_of_rows, up_matrix, preferred_element_type=jnp.float32)  5.99 us
  transfers between devices with their start and end apart: 4, of which 3 were waited for; matrix products, arithmetic and copies ran while one was open for 26% of the time, Pallas kernels for 0%

commit v1 on v0

--- a/solution.py
+++ b/solution.py
@@ -1,9 +1,17 @@
+import functools
+
 import jax
 import jax.numpy as jnp
 from jax import lax
+from jax.experimental import pallas as pl
+from jax.experimental.pallas import tpu as pltpu
 from jax.sharding import PartitionSpec as P
 
 SCALE_GROUP = 128
+LANES = 128
+INNER = 4
+VMEM_BYTES = 67_043_328
+MESH = pl.DeviceIdType.MESH
 EXP_DEV = 1
 
 
@@ -103,9 +111,343 @@
     return jnp.stack(outputs)
 
 
+def visit_order(groups):
+    return [sorted(range(groups), key=lambda other: (abs(other - own), other < own)) for own in range(groups)]
+
+
+def expert_kernel(
+    groups,
+    x_ref,
+    ids_ref,
+    share_ref,
+    gain_ref,
+    gate_hbm,
+    up_hbm,
+    down_hbm,
+    exps_ref,
+    out_ref,
+    rows,
+    gate,
+    up,
+    down,
+    scales,
+    hidden,
+    part,
+    core_in,
+    y_out,
+    y_in,
+    keep,
+    z_out,
+    z_in,
+    weight_sem,
+    rows_sent,
+    rows_got,
+    core_sent,
+    core_got,
+    y_sent,
+    y_got,
+    z_sent,
+    z_got,
+):
+    batches, dev_rows, width = x_ref.shape
+    fanout = ids_ref.shape[2]
+    units = groups * batches
+    chunk_rows = INNER * dev_rows
+    ffw = gate.shape[1]
+    me = lax.axis_index("ep")
+    core = lax.rem(me, 2)
+    row = lax.rem(lax.div(me, 2), 2)
+    place = lax.div(me, INNER)
+    here = row * 2 + core
+    sib = me + 1 - 2 * core
+    across = me + 2 - 4 * row
+    above = me + INNER
+    below = me - INNER
+    has_above = place < groups - 1
+    has_below = place > 0
+
+    weight_copies = [
+        pltpu.make_async_copy(gate_hbm.at[0], gate, weight_sem.at[0]),
+        pltpu.make_async_copy(up_hbm.at[0], up, weight_sem.at[1]),
+        pltpu.make_async_copy(down_hbm.at[0], down, weight_sem.at[2]),
+    ]
+    for copy in weight_copies:
+        copy.start()
+
+    barrier = pltpu.get_barrier_semaphore()
+
+    def greet(device):
+        pl.semaphore_signal(barrier, inc=1, device_id={"ep": device}, device_id_type=MESH)
+
+    greet(sib)
+    greet(across)
+    pl.when(has_above)(lambda: greet(above))
+    pl.when(has_below)(lambda: greet(below))
+
+    def remote(src, dst, sent, got, device):
+        return pltpu.make_async_remote_copy(
+            src_ref=src,
+            dst_ref=dst,
+            send_sem=sent,
+            recv_sem=got,
+            device_id={"ep": device},
+            device_id_type=MESH,
+        )
+
+    def rows_copy(outer, batch, inner, kind, device):
+        ref = rows.at[outer, batch, inner]
+        return remote(ref, ref, rows_sent.at[outer, batch, kind], rows_got.at[outer, batch, inner], device)
+
+    lane = lax.broadcasted_iota(jnp.int32, (dev_rows, LANES), 1)
+    for batch in range(batches):
+        values = x_ref[batch].astype(jnp.float32)
+        power = jnp.mean(values * values, axis=-1, keepdims=True)
+        normed = (values * lax.rsqrt(power + 1e-06) * gain_ref[...]).astype(jnp.bfloat16)
+        mixing = jnp.zeros((dev_rows, LANES), jnp.float32)
+        for k in range(fanout):
+            share = share_ref[batch, :, k : k + 1].astype(jnp.float32) / 64.0
+            mixing += jnp.where(ids_ref[batch, :, k : k + 1] == lane, share, 0.0)
+        rows[place, batch, here, :, :width] = normed
+        rows[place, batch, here, :, width:] = mixing.astype(jnp.bfloat16)
+        if batch == 0:
+            pl.semaphore_wait(barrier, 2 + has_above.astype(jnp.int32) + has_below.astype(jnp.int32))
+        pl.when(has_above)(lambda: rows_copy(place, batch, here, 0, above).start())
+        pl.when(has_below)(lambda: rows_copy(place, batch, here, 1, below).start())
+        rows_copy(place, batch, here, 3, across).start()
+        rows_copy(place, batch, here, 2, sib).start()
+
+    for m in range(3):
+        for j in range(ffw // SCALE_GROUP):
+            power_of = jnp.full((1, SCALE_GROUP), exps_ref[0, m, j], jnp.int32).astype(jnp.float32)
+            scales[m : m + 1, j * SCALE_GROUP : (j + 1) * SCALE_GROUP] = jnp.exp2(power_of)
+
+    table = visit_order(groups)
+
+    def unit_of(u):
+        step = lax.div(u, batches)
+        batch = lax.rem(u, batches)
+        outer = jnp.int32(0)
+        for own in range(groups):
+            for at in range(groups):
+                outer = jnp.where((place == own) & (step == at), jnp.int32(table[own][at]), outer)
+        return outer, batch
+
+    other_row = (1 - row) * 2 + core
+
+    def z_relay(u):
+        outer, batch = unit_of(u)
+        rows_copy(outer, batch, here, 0, sib).wait_recv()
+        pl.when((outer < place) & has_above)(lambda: rows_copy(outer, batch, here, 0, above).start())
+        pl.when((outer > place) & has_below)(lambda: rows_copy(outer, batch, here, 1, below).start())
+        rows_copy(outer, batch, here, 3, across).start()
+        rows_copy(outer, batch, here, 2, sib).start()
+
+    def y_relay(u):
+        outer, batch = unit_of(u)
+        rows_copy(outer, batch, other_row, 4, sib).wait_recv()
+        rows_copy(outer, batch, other_row, 4, sib).start()
+
+    def arrived(u):
+        outer, batch = unit_of(u)
+        rows_copy(outer, batch, row * 2 + 1 - core, 2, sib).wait_recv()
+        rows_copy(outer, batch, (1 - row) * 2 + 1 - core, 4, sib).wait_recv()
+
+    def compute_hidden(u):
+        outer, batch = unit_of(u)
+        block = rows[outer, batch, :, :, :width].reshape(chunk_rows, width)
+        tile = 256
+        for at in range(0, ffw, tile):
+            cols = slice(at, at + tile)
+            gated = jnp.dot(block, gate[:, cols], preferred_element_type=jnp.float32) * scales[0:1, cols]
+            upped = jnp.dot(block, up[:, cols], preferred_element_type=jnp.float32) * scales[1:2, cols]
+            hidden[:, cols] = (jax.nn.silu(gated) * upped * scales[2:3, cols]).astype(jnp.bfloat16)
+
+    def core_copy(outer, batch, which):
+        return remote(
+            part.at[outer, batch, which * 2 + 1 - core],
+            core_in.at[outer, batch, which],
+            core_sent.at[outer, batch, which],
+            core_got.at[outer, batch, which],
+            sib,
+        )
+
+    def compute_part(u):
+        outer, batch = unit_of(u)
+        mixing = rows[outer, batch, :, :, width:].reshape(chunk_rows, LANES).astype(jnp.float32)
+        wide_lane = lax.broadcasted_iota(jnp.int32, (chunk_rows, LANES), 1)
+        share = jnp.sum(jnp.where(wide_lane == me, mixing, 0.0), axis=1, keepdims=True)
+        tile = 512 if width % 512 == 0 else width
+        for at in range(0, width, tile):
+            cols = slice(at, at + tile)
+            produced = jnp.dot(hidden[...], down[:, cols], preferred_element_type=jnp.float32) * share
+            part[outer, batch, :, :, cols] = produced.astype(jnp.bfloat16).reshape(INNER, dev_rows, tile)
+        core_copy(outer, batch, 1 - row).start()
+        core_copy(outer, batch, row).start()
+
+    def y_copy(outer, batch):
+        return remote(
+            y_out.at[outer, batch],
+            y_in.at[outer, batch],
+            y_sent.at[outer, batch],
+            y_got.at[outer, batch],
+            across,
+        )
+
+    def core_reduce(u):
+        outer, batch = unit_of(u)
+        core_copy(outer, batch, 1 - row).wait_recv()
+        summed = part[outer, batch, other_row].astype(jnp.float32) + core_in[outer, batch, 1 - row].astype(jnp.float32)
+        y_out[outer, batch] = summed.astype(jnp.bfloat16)
+        y_copy(outer, batch).start()
+        core_copy(outer, batch, row).wait_recv()
+        keep[outer, batch] = part[outer, batch, here].astype(jnp.float32) + core_in[outer, batch, row].astype(
+            jnp.float32
+        )
+
+    def y_reduce(u):
+        outer, batch = unit_of(u)
+        y_copy(outer, batch).wait_recv()
+        keep[outer, batch] += y_in[outer, batch].astype(jnp.float32)
+
+    def z_copy(way, outer, batch, device):
+        return remote(
+            z_out.at[outer, batch],
+            z_in.at[way, outer, batch],
+            z_sent.at[outer, batch],
+            z_got.at[way, outer, batch],
+            device,
+        )
+
+    def chain(u):
+        step = lax.div(u, batches)
+        batch = lax.rem(u, batches)
+        for way, outer, active, more, device in (
+            (0, step, step > place, has_below, above),
+            (1, groups - 1 - step, groups - 1 - step < place, has_above, below),
+        ):
+
+            @pl.when(active & more)
+            def _():
+                z_copy(way, outer, batch, sib).wait_recv()
+                summed = keep[outer, batch] + z_in[way, outer, batch].astype(jnp.float32)
+                z_out[outer, batch] = summed.astype(jnp.bfloat16)
+                z_copy(way, outer, batch, device).start()
+
+            @pl.when(active & jnp.logical_not(more))
+            def _():
+                z_out[outer, batch] = keep[outer, batch].astype(jnp.bfloat16)
+                z_copy(way, outer, batch, device).start()
+
+    y_relay(0)
+    for copy in weight_copies:
+        copy.wait()
+
+    @pl.loop(0, units + 2)
+    def _(u):
+        @pl.when(u < units)
+        def _():
+            arrived(u)
+            compute_hidden(u)
+
+        pl.when(u + 1 < units)(lambda: y_relay(u + 1))
+        pl.when(u + batches < units)(lambda: z_relay(u + batches))
+        pl.when(u < units)(lambda: compute_part(u))
+        pl.when((u >= 1) & (u <= units))(lambda: core_reduce(u - 1))
+
+        @pl.when(u >= 2)
+        def _():
+            y_reduce(u - 2)
+            chain(u - 2)
+
+    for batch in range(batches):
+
+        @pl.when(has_below)
+        def _():
+            z_copy(0, place, batch, sib).wait_recv()
+            keep[place, batch] += z_in[0, place, batch].astype(jnp.float32)
+
+        @pl.when(has_above)
+        def _():
+            z_copy(1, place, batch, sib).wait_recv()
+            keep[place, batch] += z_in[1, place, batch].astype(jnp.float32)
+
+        out_ref[batch] = (x_ref[batch].astype(jnp.float32) + keep[place, batch]).astype(jnp.bfloat16)
+
+    @pl.loop(0, units)
+    def _(u):
+        outer = lax.div(u, batches)
+        batch = lax.rem(u, batches)
+        pl.when((outer <= place) & has_above)(lambda: rows_copy(outer, batch, here, 0, sib).wait_send())
+        pl.when((outer >= place) & has_below)(lambda: rows_copy(outer, batch, here, 1, sib).wait_send())
+        for kind in (2, 3, 4):
+            rows_copy(outer, batch, here, kind, sib).wait_send()
+        core_copy(outer, batch, 0).wait_send()
+        core_copy(outer, batch, 1).wait_send()
+        y_copy(outer, batch).wait_send()
+        pl.when(outer != place)(lambda: z_copy(0, outer, batch, sib).wait_send())
+
+
+def kernel_scratch(groups, batches, dev_rows, width, ffw):
+    block = (groups, batches)
+    bf16 = jnp.bfloat16
+    buffers = [
+        ((*block, INNER, dev_rows, width + LANES), bf16),
+        ((width, ffw), bf16),
+        ((width, ffw), bf16),
+        ((ffw, width), bf16),
+        ((8, ffw), jnp.float32),
+        ((INNER * dev_rows, ffw), bf16),
+        ((*block, INNER, dev_rows, width), bf16),
+        ((*block, 2, dev_rows, width), bf16),
+        ((*block, dev_rows, width), bf16),
+        ((*block, dev_rows, width), bf16),
+        ((*block, dev_rows, width), jnp.float32),
+        ((*block, dev_rows, width), bf16),
+        ((2, *block, dev_rows, width), bf16),
+    ]
+    semaphores = [(3,), (*block, 5), (*block, INNER), (*block, 2), (*block, 2), block, block, block, (2, *block)]
+    return buffers, semaphores
+
+
+def fused(groups, buffers, semaphores, hidden_in, expert_ids, route_share, norm_gain, gate_weight, up_weight, down_weight, exponent_table):
+    vmem = pl.BlockSpec(memory_space=pltpu.VMEM)
+    anywhere = pl.BlockSpec(memory_space=pl.ANY)
+    return pl.pallas_call(
+        functools.partial(expert_kernel, groups),
+        out_shape=jax.ShapeDtypeStruct(hidden_in.shape, hidden_in.dtype),
+        in_specs=[vmem, vmem, vmem, vmem, anywhere, anywhere, anywhere, pl.BlockSpec(memory_space=pltpu.SMEM)],
+        out_specs=vmem,
+        scratch_shapes=[pltpu.VMEM(shape, kind) for shape, kind in buffers]
+        + [pltpu.SemaphoreType.DMA(shape) for shape in semaphores],
+        compiler_params=pltpu.CompilerParams(
+            collective_id=0, has_side_effects=True, vmem_limit_bytes=VMEM_BYTES * 15 // 16
+        ),
+    )(hidden_in, expert_ids, route_share, norm_gain[None, :], gate_weight, up_weight, down_weight, exponent_table)
+
+
+def serve_local(*args):
+    hidden_in, gate_weight = args[0], args[4]
+    owners = lax.axis_size("ep")
+    batches, dev_rows, width = hidden_in.shape
+    ffw = gate_weight.shape[2]
+    groups = owners // INNER
+    if owners % INNER or owners > LANES:
+        return local(*args)
+    buffers, semaphores = kernel_scratch(groups, batches, dev_rows, width, ffw)
+    total = 0
+    for shape, kind in buffers:
+        size = jnp.dtype(kind).itemsize
+        for extent in shape:
+            size *= extent
+        total += size
+    if total > VMEM_BYTES * 3 // 4:
+        return local(*args)
+    return fused(groups, buffers, semaphores, *args)
+
+
 def solution(mesh):
     return jax.shard_map(
-        local,
+        serve_local,
         mesh=mesh,
         in_specs=(
             P(None, ("grp", "ep"), None),

time: 199 us -> 92.1 us (0.46)
  the two profiles are of different devices: /device:TPU:15 before, /device:TPU:0 now
where the time goes in v1:
time: 92.1 us; the launch traced here: 91.9 us
  Pallas kernels  86.2 us (94%)
  local copies, waits for them, and re-layouts  5.71 us (6%)
    pallas_call x1, Pallas kernels, fused(): pl.pallas_call(functools.partial(expert_kernel, groups), out_shape=jax.Sh...  86.2 us
    unnamed x4, local copies, waits for them, and re-layouts  5.71 us

profile of v1, /device:TPU:0, one launch (start us, length us, event | category | flops | bytes accessed | tf_op | source)
XLA Modules:
  0.0 91.9 jit_solution(16111257394628244639)
XLA Ops:
  0.0 1.3 %copy.11.exps_ref = s32[1,3,6]{2,1,0:T(4,128)} copy(s32[1,3,6]{2,0,1:T(1,128)} %param.15) | data formatting | bytes 144 | tf_op args[7]
  1.3 1.4 %copy.9.ids_ref = s32[2,32,8]{2,1,0:T(8,128)} copy(s32[2,32,8]{1,2,0:T(8,128)} %param.9) | data formatting | bytes 4096 | tf_op args[1]
  2.7 1.4 %copy.10.share_ref = s32[2,32,8]{2,1,0:T(8,128)} copy(s32[2,32,8]{1,2,0:T(8,128)} %param.10) | data formatting | bytes 4096 | tf_op args[2]
  4.0 86.2 %shard_map.82 = bf16[2,32,2048]{2,1,0:T(8,128)(2,1)} custom-call(bf16[2,32,2048]{2,1,0:T(8,128)(2,1)} %x_ref.1, s32[2,32,8]{2,1,0:T(8,128)} %copy.9.ids_ref, s32[2,32,8]{2,1,0:T(8,128)} %copy.10.share_ref, f32[1,2048]{1,0:T(1,128)} %bitcast.1, bf16[1,2048,768]{2,1,0:T(8,128)(2,1)} %gate_hbm.1, bf16[1,2048,768]{2,1,0:T(8,128)(2,1)} %up_hbm.1, ...), custom_call_target="tpu_custom_call" | custom-call | tf_op jit(solution)/shard_map/pallas_call | solution.py:415
  90.2 1.7 %copy.13 = bf16[2,32,2048]{2,1,0:T(8,128)(2,1)} copy(bf16[2,32,2048]{2,1,0:T(8,128)(2,1)} %shard_map.82) | data formatting | bytes 524288

commit v2 on v1

--- a/solution.py
+++ b/solution.py
@@ -111,8 +111,41 @@
     return jnp.stack(outputs)
 
 
-def visit_order(groups):
-    return [sorted(range(groups), key=lambda other: (abs(other - own), other < own)) for own in range(groups)]
+def unit_tables(groups, batches):
+    arrival, reduction = [], []
+    for own in range(groups):
+        keys = [(abs(o - own), b, o < own, o) for o in range(groups) for b in range(batches)]
+        units = [o * batches + b for _, b, _, o in sorted(keys)]
+        steps = [units[at * batches : (at + 1) * batches] for at in range(groups)]
+        late = steps[max(groups - 2, 0) :]
+        early = steps[: max(groups - 2, 0)][::-1]
+        arrival.append(units)
+        reduction.append([unit for step in late + early for unit in step])
+    chains = {}
+    last = 0
+    for way in range(2):
+        for rank in range(groups):
+            own = rank if way == 0 else groups - 1 - rank
+            dests = [o for o in range(groups) if (o > own if way == 0 else o < own)]
+            before = own - 1 if way == 0 else own + 1
+            wanted = []
+            for outer in dests:
+                for batch in range(batches):
+                    unit = outer * batches + batch
+                    ready = reduction[own].index(unit)
+                    if rank > 0:
+                        upstream = [at for at, found in chains[way, before].items() if found == unit][0]
+                        ready = max(ready, upstream + 2)
+                    wanted.append((ready, -abs(outer - own), unit))
+            taken = {}
+            for ready, _, unit in sorted(wanted):
+                while ready in taken:
+                    ready += 1
+                taken[ready] = unit
+                last = max(last, ready + 1)
+            chains[way, own] = taken
+    chain_rows = [[[chains[way, own].get(at, -1) for at in range(last)] for own in range(groups)] for way in range(2)]
+    return arrival, reduction, chain_rows, last
 
 
 def expert_kernel(
@@ -150,7 +183,7 @@
     z_got,
 ):
     batches, dev_rows, width = x_ref.shape
-    fanout = ids_ref.shape[2]
+    fanout = ids_ref.shape[1]
     units = groups * batches
     chunk_rows = INNER * dev_rows
     ffw = gate.shape[1]
@@ -198,17 +231,17 @@
         ref = rows.at[outer, batch, inner]
         return remote(ref, ref, rows_sent.at[outer, batch, kind], rows_got.at[outer, batch, inner], device)
 
-    lane = lax.broadcasted_iota(jnp.int32, (dev_rows, LANES), 1)
+    expert = lax.broadcasted_iota(jnp.int32, (LANES, dev_rows), 0)
     for batch in range(batches):
         values = x_ref[batch].astype(jnp.float32)
         power = jnp.mean(values * values, axis=-1, keepdims=True)
         normed = (values * lax.rsqrt(power + 1e-06) * gain_ref[...]).astype(jnp.bfloat16)
-        mixing = jnp.zeros((dev_rows, LANES), jnp.float32)
+        mixing = jnp.zeros((LANES, dev_rows), jnp.float32)
         for k in range(fanout):
-            share = share_ref[batch, :, k : k + 1].astype(jnp.float32) / 64.0
-            mixing += jnp.where(ids_ref[batch, :, k : k + 1] == lane, share, 0.0)
+            share = share_ref[batch, k : k + 1, :].astype(jnp.float32) / 64.0
+            mixing += jnp.where(ids_ref[batch, k : k + 1, :] == expert, share, 0.0)
         rows[place, batch, here, :, :width] = normed
-        rows[place, batch, here, :, width:] = mixing.astype(jnp.bfloat16)
+        rows[place, batch, here, :, width:] = mixing.T.astype(jnp.bfloat16)
         if batch == 0:
             pl.semaphore_wait(barrier, 2 + has_above.astype(jnp.int32) + has_below.astype(jnp.int32))
         pl.when(has_above)(lambda: rows_copy(place, batch, here, 0, above).start())
@@ -218,29 +251,41 @@
 
     for m in range(3):
         for j in range(ffw // SCALE_GROUP):
-            power_of = jnp.full((1, SCALE_GROUP), exps_ref[0, m, j], jnp.int32).astype(jnp.float32)
+            power_of = jnp.full((1, SCALE_GROUP), exps_ref[m, 0, j], jnp.int32).astype(jnp.float32)
             scales[m : m + 1, j * SCALE_GROUP : (j + 1) * SCALE_GROUP] = jnp.exp2(power_of)
 
-    table = visit_order(groups)
+    arrival, reduction, chain_rows, slots = unit_tables(groups, batches)
+
+    def look_up(table, index):
+        found = jnp.int32(-1)
+        for own in range(groups):
+            for at, unit in enumerate(table[own]):
+                found = jnp.where((place == own) & (index == at), jnp.int32(unit), found)
+        return found
+
+    def split(unit):
+        return lax.div(unit, batches), lax.rem(unit, batches)
 
     def unit_of(u):
-        step = lax.div(u, batches)
-        batch = lax.rem(u, batches)
-        outer = jnp.int32(0)
-        for own in range(groups):
-            for at in range(groups):
-                outer = jnp.where((place == own) & (step == at), jnp.int32(table[own][at]), outer)
-        return outer, batch
+        return split(look_up(arrival, u))
+
+    def reduced_unit(u):
+        return split(look_up(reduction, u))
 
     other_row = (1 - row) * 2 + core
 
-    def z_relay(u):
-        outer, batch = unit_of(u)
-        rows_copy(outer, batch, here, 0, sib).wait_recv()
-        pl.when((outer < place) & has_above)(lambda: rows_copy(outer, batch, here, 0, above).start())
-        pl.when((outer > place) & has_below)(lambda: rows_copy(outer, batch, here, 1, below).start())
-        rows_copy(outer, batch, here, 3, across).start()
-        rows_copy(outer, batch, here, 2, sib).start()
+    def z_relay(i):
+        distance = lax.div(i, batches) + 1
+        batch = lax.rem(i, batches)
+
+        def pass_on(outer, kind, more, device):
+            rows_copy(outer, batch, here, kind, sib).wait_recv()
+            pl.when(more)(lambda: rows_copy(outer, batch, here, kind, device).start())
+            rows_copy(outer, batch, here, 3, across).start()
+            rows_copy(outer, batch, here, 2, sib).start()
+
+        pl.when(place + distance < groups)(lambda: pass_on(place + distance, 1, has_below, below))
+        pl.when(place - distance >= 0)(lambda: pass_on(place - distance, 0, has_above, above))
 
     def y_relay(u):
         outer, batch = unit_of(u)
@@ -294,7 +339,7 @@
         )
 
     def core_reduce(u):
-        outer, batch = unit_of(u)
+        outer, batch = reduced_unit(u)
         core_copy(outer, batch, 1 - row).wait_recv()
         summed = part[outer, batch, other_row].astype(jnp.float32) + core_in[outer, batch, 1 - row].astype(jnp.float32)
         y_out[outer, batch] = summed.astype(jnp.bfloat16)
@@ -305,7 +350,7 @@
         )
 
     def y_reduce(u):
-        outer, batch = unit_of(u)
+        outer, batch = reduced_unit(u)
         y_copy(outer, batch).wait_recv()
         keep[outer, batch] += y_in[outer, batch].astype(jnp.float32)
 
@@ -319,12 +364,10 @@
         )
 
     def chain(u):
-        step = lax.div(u, batches)
-        batch = lax.rem(u, batches)
-        for way, outer, active, more, device in (
-            (0, step, step > place, has_below, above),
-            (1, groups - 1 - step, groups - 1 - step < place, has_above, below),
-        ):
+        for way, more, device in ((0, has_below, above), (1, has_above, below)):
+            unit = look_up(chain_rows[way], u)
+            active = unit >= 0
+            outer, batch = split(jnp.maximum(unit, 0))
 
             @pl.when(active & more)
             def _():
@@ -338,26 +381,32 @@
                 z_out[outer, batch] = keep[outer, batch].astype(jnp.bfloat16)
                 z_copy(way, outer, batch, device).start()
 
-    y_relay(0)
-    for copy in weight_copies:
-        copy.wait()
-
-    @pl.loop(0, units + 2)
-    def _(u):
-        @pl.when(u < units)
+    early = max(units - batches, 0)
+
+    @pl.loop(0, units + 1)
+    def _(i):
+        pl.when(i < (groups - 1) * batches)(lambda: z_relay(i))
+        pl.when(i < units)(lambda: y_relay(i))
+
+        @pl.when(i == 1)
         def _():
-            arrived(u)
-            compute_hidden(u)
-
-        pl.when(u + 1 < units)(lambda: y_relay(u + 1))
-        pl.when(u + batches < units)(lambda: z_relay(u + batches))
-        pl.when(u < units)(lambda: compute_part(u))
-        pl.when((u >= 1) & (u <= units))(lambda: core_reduce(u - 1))
-
-        @pl.when(u >= 2)
+            for copy in weight_copies:
+                copy.wait()
+
+        @pl.when(i >= 1)
         def _():
-            y_reduce(u - 2)
-            chain(u - 2)
+            arrived(i - 1)
+            compute_hidden(i - 1)
+            compute_part(i - 1)
+
+        pl.when(i >= early)(lambda: core_reduce(i - early))
+
+    pl.loop(units + 1 - early, units)(core_reduce)
+
+    @pl.loop(0, slots)
+    def _(k):
+        pl.when(k < units)(lambda: y_reduce(k))
+        chain(k)
 
     for batch in range(batches):
 
@@ -422,7 +471,16 @@
         compiler_params=pltpu.CompilerParams(
             collective_id=0, has_side_effects=True, vmem_limit_bytes=VMEM_BYTES * 15 // 16
         ),
-    )(hidden_in, expert_ids, route_share, norm_gain[None, :], gate_weight, up_weight, down_weight, exponent_table)
+    )(
+        hidden_in,
+        jnp.swapaxes(expert_ids, 1, 2),
+        jnp.swapaxes(route_share, 1, 2),
+        norm_gain[None, :],
+        gate_weight,
+        up_weight,
+        down_weight,
+        jnp.swapaxes(exponent_table, 0, 1),
+    )
 
 
 def serve_local(*args):
@@ -431,7 +489,7 @@
     batches, dev_rows, width = hidden_in.shape
     ffw = gate_weight.shape[2]
     groups = owners // INNER
-    if owners % INNER or owners > LANES:
+    if owners % INNER or owners > LANES or owners < 2 * INNER:
         return local(*args)
     buffers, semaphores = kernel_scratch(groups, batches, dev_rows, width, ffw)
     total = 0

time: 92.1 us -> 62.7 us (0.68)
  Pallas kernels: 86.2 us -> 60.9 us
  local copies, waits for them, and re-layouts: 5.71 us -> 1.67 us
    pallas_call x1, Pallas kernels: 86.2 us -> 60.9 us  [fused(): pl.pallas_call(functools.partial(expert_kernel, groups), out_shape=jax.Sh...]
    unnamed x4 -> x1, local copies, waits for them, and re-layouts: 5.71 us -> 1.67 us
where the time goes in v2:
time: 62.7 us; the launch traced here: 62.6 us
  Pallas kernels  60.9 us (97%)
  local copies, waits for them, and re-layouts  1.67 us (3%)
    pallas_call x1, Pallas kernels, fused(): pl.pallas_call(functools.partial(expert_kernel, groups), out_shape=jax.Sh...  60.9 us
    unnamed x1, local copies, waits for them, and re-layouts  1.67 us

profile of v2, /device:TPU:0, one launch (start us, length us, event | category | flops | bytes accessed | tf_op | source)
XLA Modules:
  0.0 62.6 jit_solution(11917303749314473912)
XLA Ops:
  0.0 60.9 %shard_map.82 = bf16[2,32,2048]{2,1,0:T(8,128)(2,1)} custom-call(bf16[2,32,2048]{2,1,0:T(8,128)(2,1)} %x_ref.1, s32[2,8,32]{2,1,0:T(8,128)} %bitcast.4, s32[2,8,32]{2,1,0:T(8,128)} %bitcast.5, f32[1,2048]{1,0:T(1,128)} %bitcast.6, bf16[1,2048,768]{2,1,0:T(8,128)(2,1)} %gate_hbm.1, bf16[1,2048,768]{2,1,0:T(8,128)(2,1)} %up_hbm.1, ...), custom_call_target="tpu_custom_call" | custom-call | tf_op jit(solution)/shard_map/pallas_call | solution.py:464
  60.9 1.7 %copy.10 = bf16[2,32,2048]{2,1,0:T(8,128)(2,1)} copy(bf16[2,32,2048]{2,1,0:T(8,128)(2,1)} %shard_map.82) | data formatting | bytes 524288

commit v3 on v2

--- a/solution.py
+++ b/solution.py
@@ -132,10 +132,10 @@
             for outer in dests:
                 for batch in range(batches):
                     unit = outer * batches + batch
-                    ready = reduction[own].index(unit)
+                    ready = 2 * reduction[own].index(unit)
                     if rank > 0:
                         upstream = [at for at, found in chains[way, before].items() if found == unit][0]
-                        ready = max(ready, upstream + 2)
+                        ready = max(ready, upstream + 3)
                     wanted.append((ready, -abs(outer - own), unit))
             taken = {}
             for ready, _, unit in sorted(wanted):
@@ -145,7 +145,7 @@
                 last = max(last, ready + 1)
             chains[way, own] = taken
     chain_rows = [[[chains[way, own].get(at, -1) for at in range(last)] for own in range(groups)] for way in range(2)]
-    return arrival, reduction, chain_rows, last
+    return arrival, reduction, chain_rows, max((last + 1) // 2, groups * batches)
 
 
 def expert_kernel(
@@ -256,21 +256,30 @@
 
     arrival, reduction, chain_rows, slots = unit_tables(groups, batches)
 
-    def look_up(table, index):
-        found = jnp.int32(-1)
-        for own in range(groups):
-            for at, unit in enumerate(table[own]):
-                found = jnp.where((place == own) & (index == at), jnp.int32(unit), found)
+    def own_row(table):
+        found = [jnp.int32(unit) for unit in table[0]]
+        for own in range(1, groups):
+            found = [jnp.where(place == own, jnp.int32(unit), kept) for unit, kept in zip(table[own], found)]
+        return found
+
+    own_arrival, own_reduction = own_row(arrival), own_row(reduction)
+
+    def look_up(row_units, index):
+        if isinstance(index, int):
+            return row_units[index] if index < len(row_units) else jnp.int32(-1)
+        found = row_units[0]
+        for at in range(1, len(row_units)):
+            found = jnp.where(index == at, row_units[at], found)
         return found
 
     def split(unit):
         return lax.div(unit, batches), lax.rem(unit, batches)
 
     def unit_of(u):
-        return split(look_up(arrival, u))
+        return split(look_up(own_arrival, u))
 
     def reduced_unit(u):
-        return split(look_up(reduction, u))
+        return split(look_up(own_reduction, u))
 
     other_row = (1 - row) * 2 + core
 
@@ -365,7 +374,9 @@
 
     def chain(u):
         for way, more, device in ((0, has_below, above), (1, has_above, below)):
-            unit = look_up(chain_rows[way], u)
+            if all(u >= len(row_units) or row_units[u] < 0 for row_units in chain_rows[way]):
+                continue
+            unit = look_up(own_row(chain_rows[way]), u)
             active = unit >= 0
             outer, batch = split(jnp.maximum(unit, 0))
 
@@ -401,12 +412,14 @@
 
         pl.when(i >= early)(lambda: core_reduce(i - early))
 
-    pl.loop(units + 1 - early, units)(core_reduce)
-
-    @pl.loop(0, slots)
-    def _(k):
-        pl.when(k < units)(lambda: y_reduce(k))
-        chain(k)
+    for k in range(units + 1 - early, units):
+        core_reduce(k)
+
+    for k in range(slots):
+        if k < units:
+            y_reduce(k)
+        chain(2 * k)
+        chain(2 * k + 1)
 
     for batch in range(batches):
 

time: 62.7 us -> 62.6 us (level)
  no operation moved by 1% of the time
where the time goes in v3:
time: 62.6 us; the launch traced here: 62.5 us
  Pallas kernels  60.8 us (97%)
  local copies, waits for them, and re-layouts  1.67 us (3%)
    pallas_call x1, Pallas kernels, fused(): pl.pallas_call(functools.partial(expert_kernel, groups), out_shape=jax.Sh...  60.8 us
    unnamed x1, local copies, waits for them, and re-layouts  1.67 us

profile of v3, /device:TPU:0, one launch (start us, length us, event | category | flops | bytes accessed | tf_op | source)
XLA Modules:
  0.0 62.5 jit_solution(12142408073712652532)
XLA Ops:
  0.0 60.8 %shard_map.82 = bf16[2,32,2048]{2,1,0:T(8,128)(2,1)} custom-call(bf16[2,32,2048]{2,1,0:T(8,128)(2,1)} %x_ref.1, s32[2,8,32]{2,1,0:T(8,128)} %bitcast.4, s32[2,8,32]{2,1,0:T(8,128)} %bitcast.5, f32[1,2048]{1,0:T(1,128)} %bitcast.6, bf16[1,2048,768]{2,1,0:T(8,128)(2,1)} %gate_hbm.1, bf16[1,2048,768]{2,1,0:T(8,128)(2,1)} %up_hbm.1, ...), custom_call_target="tpu_custom_call" | custom-call | tf_op jit(solution)/shard_map/pallas_call | solution.py:477
  60.8 1.7 %copy.10 = bf16[2,32,2048]{2,1,0:T(8,128)(2,1)} copy(bf16[2,32,2048]{2,1,0:T(8,128)(2,1)} %shard_map.82) | data formatting | bytes 524288
